TPU v7x, 512 devices: a whole 4x8x8 slice. The times are simulated.
512 devices in a mesh: row: 16 (over x, y_lo, core), col: 32 (over y_hi, z).
Axes of the slice: x: 4, y: 8 (y_hi: 4, y_lo: 2; y = y_hi * 2 + y_lo), z: 8, core: 2. Of those that a mesh axis runs over, the one named last changes fastest.
Arguments:
- features: float32 [65536, 256], P(('row', 'col')), may hold values from -6 to 6
- adj_tiles: bfloat16 [16, 32, 96, 128, 128], P('row', 'col'), may hold values from 0 to 1, as said below
- tile_dst: int32 [16, 32, 96], P('row', 'col'), may hold values from 0 to 15, as said below
- tile_src: int32 [16, 32, 96], P('row', 'col'), may hold values from 0 to 31, as said below
- tile_count: int32 [16, 32], P('row', 'col'), may hold values from 1 to 96, as said below
- self_weight: float32 [256, 256], replicated, may hold values from -0.375 to 0.375
- neighbor_weight: float32 [256, 256], replicated, may hold values from -1.5 to 1.5
- layer_bias: float32 [256], replicated, may hold values from -3 to 3
Outputs:
- activated: float32 [65536, 256], P(('row', 'col'))
Inputs may be any that keep to these rules, and one draw needn't show every extreme that they name: `adj_tiles`: every entry is 0 or 1. `tile_dst`: a destination tile within the column group of the device. `tile_src`: a source tile within the row group of the device. `tile_count`: list entries at and beyond a device's count are padding; every device holds at least one listed tile; some device holds exactly 96.
All inputs are finite; a program needn't handle non-finite values.
Results may differ from a plain program's by a relative error of at most 0.0003.
Values sent between devices are 32-bit elements; how exact they have to be, the bound alone decides.
A program may use at most 64 MiB of HBM per device.

v0:
```python
import jax
import jax.numpy as jnp
from jax import lax
from jax.sharding import PartitionSpec as P


def accumulate(blocks, source_tiles, sources, targets, valid_count, state_pair):

    def visit(group, inner_pair):
        aggregate, degrees = inner_pair
        first_slot = group * 8
        block_group = lax.dynamic_slice_in_dim(blocks, first_slot, 8, 0).astype(jnp.float32)
        source_ids = lax.dynamic_slice_in_dim(sources, first_slot, 8, 0)
        source_group = jnp.take(source_tiles, source_ids, axis=0)
        target_group = lax.dynamic_slice_in_dim(targets, first_slot, 8, 0)
        live_slots = (first_slot + jnp.arange(8, dtype=jnp.int32) < valid_count).astype(jnp.float32)
        products = jnp.einsum(
            "kij,kjf->kif", block_group, source_group, precision=lax.Precision.HIGHEST
        )
        row_sums = jnp.sum(block_group, axis=2)
        for slot in range(8):
            target_id = target_group[slot]
            current = lax.dynamic_slice_in_dim(aggregate, target_id, 1, 0)
            aggregate = lax.dynamic_update_slice_in_dim(
                aggregate, current + live_slots[slot] * products[slot][None], target_id, 0
            )
            current_deg = lax.dynamic_slice_in_dim(degrees, target_id, 1, 0)
            degrees = lax.dynamic_update_slice_in_dim(
                degrees, current_deg + live_slots[slot] * row_sums[slot][None], target_id, 0
            )
        return (aggregate, degrees)

    group_count = (valid_count + 7) // 8
    return lax.fori_loop(0, group_count, visit, state_pair)


def on_device(
    features, adj_tiles, tile_dst, tile_src, tile_count, self_weight, neighbor_weight, layer_bias
):
    tile_size = adj_tiles.shape[-1]
    feat_width = features.shape[1]
    node_rows = features.shape[0]
    adjacency = adj_tiles[0, 0]
    targets = tile_dst[0, 0]
    sources = tile_src[0, 0]
    valid_total = tile_count[0, 0]
    gathered = lax.all_gather(features, "col", axis=0, tiled=True)
    source_tiles = gathered.reshape(-1, tile_size, feat_width)
    target_count = lax.axis_size("row") * node_rows // tile_size
    start_pair = (
        jnp.zeros((target_count, tile_size, feat_width), jnp.float32),
        jnp.zeros((target_count, tile_size), jnp.float32),
    )
    state_pair = accumulate(adjacency, source_tiles, sources, targets, valid_total, start_pair)
    aggregate = state_pair[0].reshape(-1, feat_width)
    degrees = state_pair[1].reshape(-1)
    summed_rows, summed_degrees = lax.psum((aggregate, degrees), "row")
    first_row = lax.axis_index("row") * node_rows
    own_rows = lax.dynamic_slice_in_dim(summed_rows, first_row, node_rows, 0)
    own_degrees = lax.dynamic_slice_in_dim(summed_degrees, first_row, node_rows, 0)
    neighbor_mean = own_rows / jnp.maximum(own_degrees, 1.0)[:, None]
    own_part = jnp.dot(
        features, self_weight, precision=lax.Precision.HIGHEST, preferred_element_type=jnp.float32
    )
    neighbor_part = jnp.dot(
        neighbor_mean,
        neighbor_weight,
        precision=lax.Precision.HIGHEST,
        preferred_element_type=jnp.float32,
    )
    return jnp.maximum(own_part + neighbor_part + layer_bias, 0.0)


def solution(mesh):
    placed = (
        P(("row", "col"), None),
        P("row", "col", None, None, None),
        P("row", "col", None),
        P("row", "col", None),
        P("row", "col"),
        P(),
        P(),
        P(),
    )
    return jax.shard_map(
        on_device, mesh=mesh, in_specs=placed, out_specs=P(("row", "col"), None), check_vma=False
    )
```

profile of v0, /device:TPU:1, one launch (start us, length us, event | category | flops | bytes accessed | tf_op | source)
XLA Modules:
  0.0 822.1 jit_solution(7853161686528989406)
XLA Ops:
  6.5 0.0 copy-start
  6.5 0.0 copy-start.6
  6.5 0.0 copy-start.4
  6.5 0.0 all-gather.2.cloned.1.call-start
  6.5 0.7 all-gather.2.cloned.1.call-update
  7.3 0.0 all-reduce.2.cloned.1.call-start
  8.0 108.7 %all-gather.2.cloned.1.call-done = f32[4096,256]{1,0:T(8,128)} async-done(((f32[128,256]{1,0:T(8,128)}), f32[4096,256]{1,0:T(8,128)}) %all-gather.2.cloned.1.call-update) | async-done | bytes 4194320 | tf_op jit(solution)/shard_map/all_gather | solution.py:47
  116.7 1.5 broadcast_in_dim.20
  118.2 0.0 copy-done.6
  118.2 0.0 copy-done.4
  118.2 46.9 %while.12 = (s32[]{:T(128)}, f32[16,128,256]{2,1,0:T(8,128)}, f32[16,128]{1,0:T(8,128)S(1)}, s32[]{:T(128)}, s32[96]{0:T(128)S(1)}, /*index=5*/s32[]{:T(128)}, b...) while((s32[]{:T(128)}, f32[16,128,256]{2,1,0:T(8,128)}, ...), condition=%wide.region_2.3_spmd, body=%wide.region_0.2_spmd.sunk | while | flops 403703872 | bytes 12092391 | solution.py:34
  118.2 0.1 dynamic_slice.144
  118.3 0.7 fusion.66
  121.0 0.7 compare_and_fusion.2
  121.8 2.8 gather_fusion
  124.6 1.7 fusion.67
  126.3 0.0 copy-start.1
  126.3 0.8 fusion.68
  127.1 2.2 fusion.69
  131.4 0.0 copy-done.1
  131.4 2.3 fusion.70
  135.8 2.2 fusion.71
  139.6 2.3 fusion.72
  143.9 2.3 fusion.73
  148.1 2.2 fusion.74
  152.1 2.2 fusion.75
  156.3 2.3 fusion.76
  158.6 1.1 convert_reduce_fusion.2
  159.7 0.6 fusion.77
  160.3 0.7 fusion.78
  161.1 0.6 fusion.79
  161.7 0.7 fusion.80
  162.4 0.7 fusion.81
  163.1 0.6 fusion.82
  163.7 0.6 fusion.83
  164.4 0.7 fusion.84
  165.1 0.0 copy-start.2
  165.2 0.0 copy-start.3
  165.2 0.0 copy-start.5
  165.2 0.0 all-reduce.2.cloned.1.call-update
  165.2 0.0 copy-done
  165.2 0.8 copy-done.2
  166.1 0.3 fusion.39
  166.3 538.9 %psum.15 = f32[2048]{0:T(1024)S(1)} all-reduce(f32[2048]{0:T(1024)S(1)} %bitcast.61), channel_id=1, replica_groups=mesh['row'=16,'col'=32] {'row'}, use_global_device_ids=true, to_apply=%region_4.5 | all-reduce | flops 2048 | bytes 16384 | tf_op jit(solution)/shard_map/psum | solution.py:57
  705.2 0.1 dynamic-slice_maximum_fusion
  705.3 108.1 %all-reduce.2.cloned.1.call-done = f32[2048,256]{1,0:T(8,128)} async-done(((f32[2048,256]{1,0:T(8,128)}), f32[2048,256]{1,0:T(8,128)}) %all-reduce.2.cloned.1.call-update) | async-done | bytes 2097168 | tf_op jit(solution)/shard_map/psum | solution.py:57
  813.4 0.0 copy-done.3
  813.4 0.0 copy-done.5
  813.4 1.9 fusion.32
  (10 shorter events, 0.3 us)
Async XLA Ops:
  6.5 158.7 %copy-start = (f32[256,256]{1,0:T(8,128)S(1)}, f32[256,256]{1,0:T(8,128)}, u32[]{:S(2)}) copy-start(f32[256,256]{1,0:T(8,128)} %param.15) | copy-start | bytes 786436
  6.5 111.7 %copy-start.6 = (s32[1,1,96]{2,1,0:T(1,128)S(1)}, s32[1,1,96]{2,1,0:T(1,128)}, u32[]{:S(2)}) copy-start(s32[1,1,96]{2,1,0:T(1,128)} %param.12) | copy-start | bytes 1156
  6.5 111.7 %copy-start.4 = (s32[1,1,96]{2,1,0:T(1,128)S(1)}, s32[1,1,96]{2,1,0:T(1,128)}, u32[]{:S(2)}) copy-start(s32[1,1,96]{2,1,0:T(1,128)} %param.13) | copy-start | bytes 1156
  6.5 110.1 %all-gather.2.cloned.1.call-start = ((), (), s32[]{:S(2)}) async-start(), calls=%async_computation | async-start | bytes 4325376 | tf_op jit(solution)/shard_map/all_gather | solution.py:47
  7.3 806.1 %all-reduce.2.cloned.1.call-start = ((), (), s32[]{:S(2)}) async-start(), calls=%async_computation.1 | async-start | bytes 4194304 | tf_op jit(solution)/shard_map/psum | solution.py:57
  126.3 5.1 copy-start.1
  165.1 0.9 copy-start.2
  165.2 648.2 %copy-start.3 = (f32[256,256]{1,0:T(8,128)S(1)}, f32[256,256]{1,0:T(8,128)}, u32[]{:S(2)}) copy-start(f32[256,256]{1,0:T(8,128)} %param.16) | copy-start | bytes 786436
  165.2 648.2 %copy-start.5 = (f32[256]{0:T(256)S(1)}, f32[256]{0:T(256)}, u32[]{:S(2)}) copy-start(f32[256]{0:T(256)} %param.17) | copy-start | bytes 3076
Sparse Core Ops, SparseCore 0:
  10.5 106.0 all-gather.1
  165.3 648.0 all-reduce.1
where the time goes:
time: 830 us; the launch traced here: 822 us
  blocking collectives  539 us (65%)
  waiting for transfers between devices  217 us (26%)
  other arithmetic  25.1 us (3%)
  loops' own time  15.5 us (2%)
  between operations  14.1 us (2%)
    psum x1, blocking collectives, on_device(): summed_rows, summed_degrees = lax.psum((aggregate, degrees), 'row')  539 us
    all_gather x1, waiting for transfers between devices, on_device(): gathered = lax.all_gather(features, 'col', axis=0, tiled=True)  109 us
    psum x1, waiting for transfers between devices, on_device(): summed_rows, summed_degrees = lax.psum((aggregate, degrees), 'row')  108 us
    dynamic_update_slice x8, other arithmetic, visit(): lax.dynamic_update_slice_in_dim(aggregate, current + live_slots[slot] * p...  18.1 us
  transfers between devices with their start and end apart: 2, of which 2 were waited for; matrix products, arithmetic and copies ran while one was open for 0% of the time, Pallas kernels for 0%

commit v1 on v0

v1 whole, which is shorter than its diff:
```python
import functools

import jax
import jax.numpy as jnp
from jax import lax
from jax.experimental import pallas as pl
from jax.experimental.pallas import tpu as pltpu
from jax.sharding import PartitionSpec as P

MESH = pl.DeviceIdType.MESH
NY, NZ = 4, 8
NX, NL, NC = 4, 2, 2
TILE, SLOTS, DSTS = 128, 96, 16
WIDE = 128
DEG = 8
SPLIT = 80
PARTS = ((0, SPLIT), (SPLIT, TILE - SPLIT))
PLUS, MINUS = 1, -1


def relays(chunk):
    found = []
    far = PLUS if chunk % 2 == 0 else MINUS
    base = {0: 0, 1: 1, 3: 1, 2: 2}
    for dy in (0, 3, 1, 2):
        sends = [(0, PLUS), (0, MINUS)]
        if dy == 0:
            sends = [(PLUS, 0), (MINUS, 0)] + sends
        if dy == 3 and far == PLUS:
            sends = [(PLUS, 0)] + sends
        if dy == 1 and far == MINUS:
            sends = [(MINUS, 0)] + sends
        found.append((base[dy], 0, 0, dy, 0, sends))
        up = 4 if dy in (0, 1) else 3
        for way, reach in ((PLUS, up), (MINUS, NZ - 1 - up)):
            for hop in range(1, reach + 1):
                sends = [(0, way)] if hop < reach else []
                found.append((base[dy] + hop, 1, 0, dy, (-way * hop) % NZ, sends))
    up = 4 if chunk % 2 == 0 else 3
    hops = [(0, 0, 0)]
    for way, reach in ((PLUS, up), (MINUS, NZ - 1 - up)):
        hops += [(way, hop, reach) for hop in range(1, reach + 1)]
    for way, hop, reach in hops:
        dz = (-way * hop) % NZ
        sends = [(PLUS, 0), (MINUS, 0)]
        if hop == 0:
            sends = [(0, PLUS), (0, MINUS)] + sends
        elif hop < reach:
            sends = [(0, way)] + sends
        found.append((hop, 0, 1, 0, dz, sends))
        out = PLUS if dz % 2 == 0 else MINUS
        found.append((hop + 1, 2, 1, 3, dz, [(PLUS, 0)] if out == PLUS else []))
        found.append((hop + 1, 2, 1, 1, dz, [(MINUS, 0)] if out == MINUS else []))
        found.append((hop + 2, 2, 1, 2, dz, []))
    rounds = [[] for _ in range(max(f[0] for f in found) + 1)]
    for f in sorted(found, key=lambda f: f[:2]):
        rounds[f[0]].append(f[2:])
    return rounds


def kernel(
    key_ref, cnt_ref, feat_ref, adj_hbm, ws_ref, wn_ref, bias_ref, out_ref,
    gath0, gath1, adj, cbuf, abuf, sbuf, got1, mine, got2, own,
    ssem, rsem, adj_sem, s1, q1, s2, q2,
):
    gath = (gath0, gath1)
    row, col = lax.axis_index("row"), lax.axis_index("col")
    y, z = col // NZ, lax.rem(col, NZ)
    x, lo, core = row // (NL * NC), lax.rem(row // NC, NL), lax.rem(row, NC)

    def col_at(dy, dz):
        return lax.rem(y + dy % NY, NY) * NZ + lax.rem(z + dz % NZ, NZ)

    def row_at(dx, dl):
        return (lax.rem(x + dx, NX) * NL + lax.rem(lo + dl, NL)) * NC + core

    sibling = row + 1 - 2 * core
    near = [(row, col_at(*e)) for e in ((1, 0), (-1, 0), (0, 1), (0, -1))]
    others = [(dx, dl) for dx in (2, 1, 3, 0) for dl in (1, 0) if (dx, dl) != (0, 0)]
    peers = near + [(sibling, col)] + [(row_at(*o), col) for o in others]

    fetch = pltpu.make_async_copy(adj_hbm, adj, adj_sem)
    fetch.start()
    for c in range(2):
        gath[c][col] = feat_ref[:, c * WIDE : (c + 1) * WIDE]

    barrier = pltpu.get_barrier_semaphore()
    for peer in peers:
        pl.semaphore_signal(barrier, inc=1, device_id=peer, device_id_type=MESH)
    pl.semaphore_wait(barrier, len(peers))

    started = []

    def piece(c, part, dy, dz, ey, ez, slot):
        first, size = PARTS[part]
        view = gath[c].at[col_at(dy, dz), pl.ds(first, size)]
        lands = ((c * 2 + part) * NY + (dy - ey) % NY) * NZ + (dz - ez) % NZ
        return pltpu.make_async_remote_copy(
            src_ref=view, dst_ref=view, send_sem=ssem.at[slot], recv_sem=rsem.at[lands],
            device_id=(row, col_at(ey, ez)), device_id_type=MESH,
        )

    plan = [relays(c) for c in range(2)]

    def relay(c, t):
        for part, dy, dz, sends in plan[c][t]:
            if not sends:
                continue
            if t:
                piece(c, part, dy, dz, 0, 0, 0).wait_recv()
            for ey, ez in sends:
                copy = piece(c, part, dy, dz, ey, ez, len(started))
                copy.start()
                started.append(copy)

    def arrive(c):
        for t, entries in enumerate(plan[c]):
            for part, dy, dz, sends in entries:
                if t and not sends:
                    piece(c, part, dy, dz, 0, 0, 0).wait_recv()

    def is_first(k):
        before = key_ref[jnp.maximum(k - 1, 0)]
        return (k == 0) | ((key_ref[k] >> 12) != (before >> 12))

    def degrees():
        fetch.wait()

        def add(k, acc):
            tile = adj[key_ref[k] & 127].astype(jnp.float32)
            acc = jnp.where(is_first(k), 0.0, acc) + tile
            abuf[k] = acc.astype(jnp.bfloat16)
            return acc

        lax.fori_loop(0, SLOTS, add, jnp.zeros((TILE, TILE), jnp.float32))
        ones = jnp.ones((DEG, TILE), jnp.bfloat16)

        def count(d, _):
            held, before = cnt_ref[d + 1], cnt_ref[d]
            tile = abuf[jnp.maximum(held - 1, 0)]
            deg = lax.dot_general(
                ones, tile, (((1,), (1,)), ((), ())), preferred_element_type=jnp.float32
            )
            sbuf[0, d // 2, lax.rem(d, 2), TILE:, :] = jnp.where(held > before, deg, 0.0)
            return 0

        lax.fori_loop(0, DSTS, count, 0)

    def own_part():
        own[...] = bias_ref[...] + jnp.dot(
            feat_ref[...], ws_ref[...], precision=lax.Precision.HIGHEST,
            preferred_element_type=jnp.float32,
        )

    def multiply(c, k0, k1, acc):
        def step(k, acc):
            key = key_ref[k]
            wide = gath[c][(key >> 7) & 31]
            high = wide.astype(jnp.bfloat16)
            low = (wide - high.astype(jnp.float32)).astype(jnp.bfloat16)
            both = jnp.concatenate([high, low], axis=1)
            prod = jnp.dot(adj[key & 127], both, preferred_element_type=jnp.float32)
            acc = jnp.where(is_first(k), 0.0, acc) + (prod[:, :WIDE] + prod[:, WIDE:])
            cbuf[k] = acc
            return acc

        return lax.fori_loop(k0, k1, step, acc, unroll=2)

    def rows_of(c):
        return TILE + (DEG if c == 0 else 0)

    def swap(c, half):
        return pltpu.make_async_remote_copy(
            src_ref=sbuf.at[c, pl.ds(half * 4, 4), 1 - core, pl.ds(0, rows_of(c))],
            dst_ref=got1.at[c, pl.ds(half * 4, 4), pl.ds(0, rows_of(c))],
            send_sem=s1.at[c * 2 + half], recv_sem=q1.at[c * 2 + half],
            device_id=(sibling, col), device_id_type=MESH,
        )

    def give(c, dx, dl):
        at = lax.rem(x + dx, NX) * NL + lax.rem(lo + dl, NL)
        n = dx * NL + dl
        return pltpu.make_async_remote_copy(
            src_ref=mine.at[c, at, pl.ds(0, rows_of(c))],
            dst_ref=got2.at[c, n, pl.ds(0, rows_of(c))],
            send_sem=s2.at[c * 8 + n], recv_sem=q2.at[c * 8 + n],
            device_id=(row_at(dx, dl), col), device_id_type=MESH,
        )

    def collect(c):
        def take(d, _):
            held, before = cnt_ref[d + 1], cnt_ref[d]
            tile = cbuf[jnp.maximum(held - 1, 0)]
            sbuf[c, d // 2, lax.rem(d, 2), :TILE, :] = jnp.where(held > before, tile, 0.0)
            return 0

        for half in range(2):
            lax.fori_loop(half * 8, half * 8 + 8, take, 0)
            swap(c, half).start()

    def spread(c):
        n = rows_of(c)
        for half in range(2):
            swap(c, half).wait_recv()
            for j in range(half * 4, half * 4 + 4):
                mine[c, j, :n] = sbuf[c, j, core, :n] + got1[c, j, :n]
        for dx, dl in others:
            give(c, dx, dl).start()

    def finish(c, scale):
        n = rows_of(c)
        total = mine[c, x * NL + lo, :n]
        for dx, dl in reversed(others):
            give(c, dx, dl).wait_recv()
            total = total + got2[c, dx * NL + dl, :n]
        if c == 0:
            deg = jnp.maximum(total[TILE : TILE + 1], 1.0)
            scale = jnp.broadcast_to(deg, (TILE, TILE)).T
        mean = total[:TILE] / scale
        own[...] += jnp.dot(
            mean, wn_ref[c * WIDE : (c + 1) * WIDE], precision=lax.Precision.HIGHEST,
            preferred_element_type=jnp.float32,
        )
        return scale

    zero = jnp.zeros((TILE, WIDE), jnp.float32)
    relay(0, 0)
    relay(1, 0)
    own_part()
    relay(0, 1)
    degrees()
    relay(0, 2)
    relay(1, 1)
    relay(0, 3)
    relay(1, 2)
    relay(0, 4)
    relay(0, 5)
    relay(0, 6)
    relay(1, 3)
    arrive(0)
    acc = multiply(0, 0, 32, zero)
    relay(1, 4)
    acc = multiply(0, 32, 64, acc)
    relay(1, 5)
    acc = multiply(0, 64, 96, acc)
    relay(1, 6)
    collect(0)
    spread(0)
    arrive(1)
    multiply(1, 0, 96, zero)
    collect(1)
    scale = finish(0, None)
    spread(1)
    finish(1, scale)
    out_ref[...] = jnp.maximum(own[...], 0.0)
    for copy in started:
        copy.wait_send()
    for c in range(2):
        for half in range(2):
            swap(c, half).wait_send()
        for dx, dl in others:
            give(c, dx, dl).wait_send()


def tables(dst, src, count):
    slot = jnp.arange(SLOTS, dtype=jnp.int32)
    key = jnp.where(slot < count, dst, DSTS) * 4096 + src * 128 + slot
    rank = jnp.sum((key[None, :] < key[:, None]).astype(jnp.int32), axis=1)
    spot = rank[:, None] == slot[None, :]
    ordered = jnp.sum(jnp.where(spot, key[:, None], 0), axis=0)
    place = jnp.arange(DSTS + 1, dtype=jnp.int32) * 4096
    counts = jnp.sum((key[:, None] < place[None, :]).astype(jnp.int32), axis=0)
    return ordered, counts


def on_device(features, adj_tiles, tile_dst, tile_src, tile_count, self_weight, neighbor_weight, layer_bias):
    ordered, counts = tables(tile_dst[0, 0], tile_src[0, 0], tile_count[0, 0])
    sends = sum(len(e[3]) for c in range(2) for r in relays(c) for e in r)
    smem = pl.BlockSpec(memory_space=pltpu.SMEM)
    vmem = pl.BlockSpec(memory_space=pltpu.VMEM)
    dma = pltpu.SemaphoreType.DMA
    f32, bf16 = jnp.float32, jnp.bfloat16
    return pl.pallas_call(
        kernel,
        out_shape=jax.ShapeDtypeStruct((TILE, 2 * WIDE), f32),
        in_specs=[smem, smem, vmem, pl.BlockSpec(memory_space=pl.ANY), vmem, vmem, vmem],
        out_specs=vmem,
        scratch_shapes=[
            pltpu.VMEM((NY * NZ, TILE, WIDE), f32),
            pltpu.VMEM((NY * NZ, TILE, WIDE), f32),
            pltpu.VMEM((SLOTS, TILE, TILE), bf16),
            pltpu.VMEM((SLOTS, TILE, WIDE), f32),
            pltpu.VMEM((SLOTS, TILE, TILE), bf16),
            pltpu.VMEM((2, NX * NL, NC, TILE + DEG, WIDE), f32),
            pltpu.VMEM((2, NX * NL, TILE + DEG, WIDE), f32),
            pltpu.VMEM((2, NX * NL, TILE + DEG, WIDE), f32),
            pltpu.VMEM((2, NX * NL, TILE + DEG, WIDE), f32),
            pltpu.VMEM((TILE, 2 * WIDE), f32),
            dma((sends,)), dma((4 * NY * NZ,)), dma,
            dma((4,)), dma((4,)), dma((16,)), dma((16,)),
        ],
        compiler_params=pltpu.CompilerParams(
            collective_id=0, has_side_effects=True, vmem_limit_bytes=48 * 1024 * 1024
        ),
        name="sage_layer",
    )(ordered, counts, features, adj_tiles[0, 0], self_weight, neighbor_weight, layer_bias[None])


def solution(mesh):
    placed = (
        P(("row", "col"), None),
        P("row", "col", None, None, None),
        P("row", "col", None),
        P("row", "col", None),
        P("row", "col"),
        P(),
        P(),
        P(),
    )
    return jax.shard_map(
        on_device, mesh=mesh, in_specs=placed, out_specs=P(("row", "col"), None), check_vma=False
    )
```

time: 830 us -> 86.7 us (0.10)
  blocking collectives: 539 us -> 0 us
  waiting for transfers between devices: 217 us -> 0 us
  Pallas kernels: 0 us -> 78.1 us
  other arithmetic: 25.1 us -> 1.15 us
  loops' own time: 15.5 us -> 0 us
  between operations: 14.1 us -> 0.68 us
    psum x1 -> x0, blocking collectives: 539 us -> none  [on_device(): summed_rows, summed_degrees = lax.psum((aggregate, degrees), 'row')]
    all_gather x1 -> x0, waiting for transfers between devices: 109 us -> none  [on_device(): gathered = lax.all_gather(features, 'col', axis=0, tiled=True)]
    psum x1 -> x0, waiting for transfers between devices: 108 us -> none  [on_device(): summed_rows, summed_degrees = lax.psum((aggregate, degrees), 'row')]
    pallas_call x0 -> x1, Pallas kernels: none -> 78.1 us  [on_device(): pl.pallas_call(kernel, out_shape=jax.ShapeDtypeStruct((TILE, 2 * WIDE), f...]
    dynamic_update_slice x8 -> x0, other arithmetic: 18.1 us -> none  [visit(): lax.dynamic_update_slice_in_dim(aggregate, current + live_slots[slot] * p...]
    another operation x1 -> x0, loops' own time: 15.5 us -> none  [accumulate(): return lax.fori_loop(0, group_count, visit, state_pair)]
  transfers between devices with their start and end apart: 2 -> 0, of which waited for: 2 -> 0; matrix products, arithmetic and copies ran while one was open for 0% -> 0% of each run, Pallas kernels for 0% -> 0%
where the time goes in v1:
time: 86.7 us; the launch traced here: 86 us
  Pallas kernels  78.1 us (90%)
  local copies, waits for them, and re-layouts  6.03 us (7%)
  other arithmetic  1.15 us (1%)
    pallas_call x1, Pallas kernels, on_device(): pl.pallas_call(kernel, out_shape=jax.ShapeDtypeStruct((TILE, 2 * WIDE), f...  78.1 us
    unnamed x11, local copies, waits for them, and re-layouts  6.03 us

profile of v1, /device:TPU:1, one launch (start us, length us, event | category | flops | bytes accessed | tf_op | source)
XLA Modules:
  0.0 86.0 jit_solution(11511152583846753316)
XLA Ops:
  0.7 0.7 iota_add_fusion
  1.3 0.2 convert_reduce_fusion
  1.5 0.1 select_reduce_fusion.key_ref
  1.6 0.2 convert_reduce_fusion.1.cnt_ref
  1.8 0.0 copy-start
  1.8 1.9 %copy-done = bf16[1,1,96,128,128]{4,3,2,1,0:T(8,128)(2,1)S(1)} copy-done((bf16[1,1,96,128,128]{4,3,2,1,0:T(8,128)(2,1)S(1)}, bf16[1,1,96,128,128]{4,3,2,1,0:T(8,128)(2,1)}, u32[]{:S(2)}) %copy-start) | copy-done | bytes 3145752
  3.7 0.0 copy-start.1
  3.7 0.9 %copy-done.1 = f32[256,256]{1,0:T(8,128)S(1)} copy-done((f32[256,256]{1,0:T(8,128)S(1)}, f32[256,256]{1,0:T(8,128)}, u32[]{:S(2)}) %copy-start.1) | copy-done | bytes 262168
  4.7 0.0 copy-start.2
  4.7 0.9 %copy-done.2 = f32[256,256]{1,0:T(8,128)S(1)} copy-done((f32[256,256]{1,0:T(8,128)S(1)}, f32[256,256]{1,0:T(8,128)}, u32[]{:S(2)}) %copy-start.2) | copy-done | bytes 262168
  5.6 0.0 copy-start.3
  5.6 0.9 %copy-done.3 = f32[128,256]{1,0:T(8,128)S(1)} copy-done((f32[128,256]{1,0:T(8,128)S(1)}, f32[128,256]{1,0:T(8,128)}, u32[]{:S(2)}) %copy-start.3) | copy-done | bytes 131096
  6.5 0.0 copy-start.4
  6.5 0.7 copy-done.4
  7.2 78.1 %sage_layer.1 = f32[128,256]{1,0:T(8,128)S(1)} custom-call(s32[96]{0:T(128)S(1)} %select_reduce_fusion.key_ref, s32[17]{0:T(128)S(1)} %convert_reduce_fusion.1.cnt_ref, f32[128,256]{1,0:T(8,128)S(1)} %copy-done.3, bf16[96,128,128]{2,1,0:T(8,128)(2,1)S(1)} %bitcast.12, f32[256,256]{1,0:T(8,128)S(1)} %copy-done.1, f32[256,256]{1,0:T(8,128)S(1)} %copy-done.2, ...), custom_call_target="tpu_custom_call" | custom-call | tf_op jit(solution)/shard_map/sage_layer/pallas_call | solution.py:283
  85.3 0.7 copy.11
  (1 shorter events, 0.0 us)
Async XLA Ops:
  1.8 1.9 %copy-start = (bf16[1,1,96,128,128]{4,3,2,1,0:T(8,128)(2,1)S(1)}, bf16[1,1,96,128,128]{4,3,2,1,0:T(8,128)(2,1)}, u32[]{:S(2)}) copy-start(bf16[1,1,96,128,128]{4,3,2,1,0:T(8,128)(2,1)} %param.9) | copy-start | bytes 9437188
  3.7 0.9 %copy-start.1 = (f32[256,256]{1,0:T(8,128)S(1)}, f32[256,256]{1,0:T(8,128)}, u32[]{:S(2)}) copy-start(f32[256,256]{1,0:T(8,128)} %ws_ref.1) | copy-start | bytes 786436
  4.7 0.9 %copy-start.2 = (f32[256,256]{1,0:T(8,128)S(1)}, f32[256,256]{1,0:T(8,128)}, u32[]{:S(2)}) copy-start(f32[256,256]{1,0:T(8,128)} %wn_ref.1) | copy-start | bytes 786436
  5.6 0.9 %copy-start.3 = (f32[128,256]{1,0:T(8,128)S(1)}, f32[128,256]{1,0:T(8,128)}, u32[]{:S(2)}) copy-start(f32[128,256]{1,0:T(8,128)} %feat_ref.1) | copy-start | bytes 393220
  6.5 0.7 copy-start.4

commit v2 on v1

v2 whole, which is shorter than its diff:
```python
import functools

import jax
import jax.numpy as jnp
from jax import lax
from jax.experimental import pallas as pl
from jax.experimental.pallas import tpu as pltpu
from jax.sharding import PartitionSpec as P

MESH = pl.DeviceIdType.MESH
NY, NZ = 4, 8
NX, NL, NC = 4, 2, 2
TILE, SLOTS, DSTS = 128, 96, 16
WIDE = 128
UNITS = ((0, 0, 128), (1, 0, 64), (1, 64, 64))
DEG = 8
SPLITS = (80, 88)
PLUS, MINUS = 1, -1


def relays(chunk):
    found = []
    far = PLUS if chunk % 2 == 0 else MINUS
    base = {0: 0, 1: 1, 3: 1, 2: 2}
    for dy in (0, 3, 1, 2):
        sends = [(0, PLUS), (0, MINUS)]
        if dy == 0:
            sends = [(PLUS, 0), (MINUS, 0)] + sends
        if dy == 3 and far == PLUS:
            sends = [(PLUS, 0)] + sends
        if dy == 1 and far == MINUS:
            sends = [(MINUS, 0)] + sends
        found.append((base[dy], 0, 0, dy, 0, sends))
        up = 4 if dy in (0, 1) else 3
        for way, reach in ((PLUS, up), (MINUS, NZ - 1 - up)):
            for hop in range(1, reach + 1):
                sends = [(0, way)] if hop < reach else []
                found.append((base[dy] + hop, 1, 0, dy, (-way * hop) % NZ, sends))
    up = 4 if chunk % 2 == 0 else 3
    hops = [(0, 0, 0)]
    for way, reach in ((PLUS, up), (MINUS, NZ - 1 - up)):
        hops += [(way, hop, reach) for hop in range(1, reach + 1)]
    for way, hop, reach in hops:
        dz = (-way * hop) % NZ
        sends = [(PLUS, 0), (MINUS, 0)]
        if hop == 0:
            sends = [(0, PLUS), (0, MINUS)] + sends
        elif hop < reach:
            sends = [(0, way)] + sends
        found.append((hop, 0, 1, 0, dz, sends))
        out = PLUS if dz % 2 == 0 else MINUS
        found.append((hop + 1, 2, 1, 3, dz, [(PLUS, 0)] if out == PLUS else []))
        found.append((hop + 1, 2, 1, 1, dz, [(MINUS, 0)] if out == MINUS else []))
        found.append((hop + 2, 2, 1, 2, dz, []))
    rounds = [[] for _ in range(max(f[0] for f in found) + 1)]
    for f in sorted(found, key=lambda f: f[:2]):
        rounds[f[0]].append(f[2:])
    return rounds


def kernel(
    feat_hbm, adj_hbm, dst_hbm, src_hbm, count_hbm, ws_hbm, wn_hbm, bias_hbm, out_ref,
    gath0, gath1, adj, cbuf, abuf, sbuf, got1, mine, got2, own,
    ws_ref, wn_ref, bias_ref, dst_ref, src_ref, count_ref, rows_ref, table,
    ssem, rsem, in_sem, s1, q1, s2, q2,
):
    gath = (gath0, gath1)
    row, col = lax.axis_index("row"), lax.axis_index("col")
    y, z = col // NZ, lax.rem(col, NZ)
    x, lo, core = row // (NL * NC), lax.rem(row // NC, NL), lax.rem(row, NC)

    def col_at(dy, dz):
        return lax.rem(y + dy % NY, NY) * NZ + lax.rem(z + dz % NZ, NZ)

    def row_at(dx, dl):
        return (lax.rem(x + dx, NX) * NL + lax.rem(lo + dl, NL)) * NC + core

    sibling = row + 1 - 2 * core
    near = [(row, col_at(*e)) for e in ((1, 0), (-1, 0), (0, 1), (0, -1))]
    others = [(dx, dl) for dx in (2, 1, 3, 0) for dl in (1, 0) if (dx, dl) != (0, 0)]
    peers = near + [(sibling, col)] + [(row_at(*o), col) for o in others]

    fetches = [
        pltpu.make_async_copy(src, dst, in_sem.at[n])
        for n, (src, dst) in enumerate((
            (feat_hbm.at[:, pl.ds(0, WIDE)], gath0.at[col]),
            (feat_hbm.at[:, pl.ds(WIDE, WIDE)], gath1.at[col]),
            (dst_hbm.at[0], dst_ref),
            (src_hbm.at[0], src_ref),
            (count_hbm, count_ref),
            (adj_hbm.at[0, 0], adj),
            (ws_hbm, ws_ref),
            (wn_hbm, wn_ref),
            (bias_hbm, bias_ref),
        ))
    ]
    for fetch in fetches:
        fetch.start()

    barrier = pltpu.get_barrier_semaphore()
    for peer in peers:
        pl.semaphore_signal(barrier, inc=1, device_id=peer, device_id_type=MESH)
    pl.semaphore_wait(barrier, len(peers))

    for fetch in fetches[:2]:
        fetch.wait()
    started = []

    def piece(c, part, dy, dz, ey, ez, slot):
        first, size = ((0, SPLITS[c]), (SPLITS[c], TILE - SPLITS[c]))[part]
        view = gath[c].at[col_at(dy, dz), pl.ds(first, size)]
        lands = ((c * 2 + part) * NY + (dy - ey) % NY) * NZ + (dz - ez) % NZ
        return pltpu.make_async_remote_copy(
            src_ref=view, dst_ref=view, send_sem=ssem.at[slot], recv_sem=rsem.at[lands],
            device_id=(row, col_at(ey, ez)), device_id_type=MESH,
        )

    plan = [relays(c) for c in range(2)]

    def relay(c, t):
        for part, dy, dz, sends in plan[c][t]:
            if not sends:
                continue
            if t:
                piece(c, part, dy, dz, 0, 0, 0).wait_recv()
            for ey, ez in sends:
                copy = piece(c, part, dy, dz, ey, ez, len(started))
                copy.start()
                started.append(copy)

    def arrive(c):
        for t, entries in enumerate(plan[c]):
            for part, dy, dz, sends in entries:
                if t and not sends:
                    piece(c, part, dy, dz, 0, 0, 0).wait_recv()

    def tables():
        for fetch in fetches[2:5]:
            fetch.wait()
        lane = lax.broadcasted_iota(jnp.int32, (1, SLOTS), 1)
        keys = jnp.where(lane < count_ref[0, 0], dst_ref[...], DSTS) * 4096
        keys = jnp.broadcast_to(keys + src_ref[...] * 128 + lane, (SLOTS, SLOTS))
        down = lax.broadcasted_iota(jnp.int32, (SLOTS, SLOTS), 0)
        across = lax.broadcasted_iota(jnp.int32, (SLOTS, SLOTS), 1)
        key = jnp.sum(jnp.where(down == across, keys, 0), axis=1, keepdims=True)
        rank = jnp.sum((keys < key).astype(jnp.int32), axis=1, keepdims=True)
        spread = jnp.where(rank == across, key, 0)
        rows_ref[0:1, 0:SLOTS] = jnp.sum(spread, axis=0, keepdims=True)
        below = (key < across * 4096).astype(jnp.int32)
        rows_ref[1:2, 0:SLOTS] = jnp.sum(below, axis=0, keepdims=True)
        copy = pltpu.make_async_copy(rows_ref, table, in_sem.at[9])
        copy.start()
        copy.wait()
        fetches[5].wait()

    def is_first(k):
        before = table[0, jnp.maximum(k - 1, 0)]
        return (k == 0) | ((table[0, k] >> 12) != (before >> 12))

    def sum_tiles(k0, k1, acc):
        def add(k, acc):
            tile = adj[table[0, k] & 127].astype(jnp.float32)
            acc = jnp.where(is_first(k), 0.0, acc) + tile
            abuf[k] = acc.astype(jnp.bfloat16)
            return acc

        return lax.fori_loop(k0, k1, add, acc, unroll=8)

    def degrees(d0, d1):
        ones = jnp.ones((DEG, TILE), jnp.bfloat16)

        def count(d, _):
            held, before = table[1, d + 1], table[1, d]
            tile = abuf[jnp.maximum(held - 1, 0)]
            deg = lax.dot_general(
                ones, tile, (((1,), (1,)), ((), ())), preferred_element_type=jnp.float32
            )
            sbuf[0, d // 2, lax.rem(d, 2), TILE:, :] = jnp.where(held > before, deg, 0.0)
            return 0

        lax.fori_loop(d0, d1, count, 0, unroll=8)

    def own_part():
        for fetch in fetches[6:]:
            fetch.wait()
        mine_in = jnp.concatenate([gath0[col], gath1[col]], axis=1)
        own[...] = bias_ref[...].reshape(1, 2 * WIDE) + jnp.dot(
            mine_in, ws_ref[...], precision=lax.Precision.HIGHEST,
            preferred_element_type=jnp.float32,
        )

    def multiply(u, k0, k1, acc):
        c, first, size = UNITS[u]

        def step(k, acc):
            key = table[0, k]
            wide = gath[c][(key >> 7) & 31]
            high = wide.astype(jnp.bfloat16)
            low = (wide - high.astype(jnp.float32)).astype(jnp.bfloat16)
            both = jnp.concatenate([high, low], axis=1)
            tile = adj[key & 127, first : first + size]
            prod = jnp.dot(tile, both, preferred_element_type=jnp.float32)
            acc = jnp.where(is_first(k), 0.0, acc) + (prod[:, :WIDE] + prod[:, WIDE:])
            cbuf[k, first : first + size] = acc
            return acc

        return lax.fori_loop(k0, k1, step, acc, unroll=16)

    def span(u):
        return UNITS[u][1], UNITS[u][2] + (DEG if u == 0 else 0)

    def swap(u, half):
        c, (first, n) = UNITS[u][0], span(u)
        return pltpu.make_async_remote_copy(
            src_ref=sbuf.at[c, pl.ds(half * 4, 4), 1 - core, pl.ds(first, n)],
            dst_ref=got1.at[c, pl.ds(half * 4, 4), pl.ds(first, n)],
            send_sem=s1.at[u * 2 + half], recv_sem=q1.at[u * 2 + half],
            device_id=(sibling, col), device_id_type=MESH,
        )

    def give(u, dx, dl):
        c, (first, n) = UNITS[u][0], span(u)
        at = lax.rem(x + dx, NX) * NL + lax.rem(lo + dl, NL)
        slot = dx * NL + dl
        return pltpu.make_async_remote_copy(
            src_ref=mine.at[c, at, pl.ds(first, n)],
            dst_ref=got2.at[c, slot, pl.ds(first, n)],
            send_sem=s2.at[u * 8 + slot], recv_sem=q2.at[u * 8 + slot],
            device_id=(row_at(dx, dl), col), device_id_type=MESH,
        )

    def collect(u):
        c, first, size = UNITS[u]

        def take(d, _):
            held, before = table[1, d + 1], table[1, d]
            tile = cbuf[jnp.maximum(held - 1, 0), first : first + size]
            tile = jnp.where(held > before, tile, 0.0)
            sbuf[c, d // 2, lax.rem(d, 2), first : first + size, :] = tile
            return 0

        for half in range(2):
            lax.fori_loop(half * 8, half * 8 + 8, take, 0)
            swap(u, half).start()

    def spread(u):
        c, (first, n) = UNITS[u][0], span(u)
        end = first + n
        for half in range(2):
            swap(u, half).wait_recv()
            for j in range(half * 4, half * 4 + 4):
                mine[c, j, first:end] = sbuf[c, j, core, first:end] + got1[c, j, first:end]
        for dx, dl in others:
            give(u, dx, dl).start()

    def finish(u, scale):
        c, (first, n) = UNITS[u][0], span(u)
        size, end = UNITS[u][2], first + n
        total = mine[c, x * NL + lo, first:end]
        for dx, dl in reversed(others):
            give(u, dx, dl).wait_recv()
            total = total + got2[c, dx * NL + dl, first:end]
        if u == 0:
            deg = jnp.maximum(total[TILE : TILE + 1], 1.0)
            scale = jnp.broadcast_to(deg, (TILE, TILE)).T
        mean = total[:size] / scale[first : first + size]
        own[first : first + size] += jnp.dot(
            mean, wn_ref[c * WIDE : (c + 1) * WIDE], precision=lax.Precision.HIGHEST,
            preferred_element_type=jnp.float32,
        )
        return scale

    zero = jnp.zeros((TILE, WIDE), jnp.float32)
    relay(0, 0)
    relay(1, 0)
    tables()
    relay(0, 1)
    relay(1, 1)
    own_part()
    relay(0, 2)
    acc = sum_tiles(0, 48, zero)
    relay(1, 2)
    sum_tiles(48, 96, acc)
    relay(0, 3)
    degrees(0, 8)
    relay(1, 3)
    degrees(8, 16)
    relay(0, 4)
    relay(0, 5)
    relay(1, 4)
    relay(0, 6)
    arrive(0)
    acc = multiply(0, 0, 48, zero)
    relay(1, 5)
    multiply(0, 48, 96, acc)
    relay(1, 6)
    collect(0)
    spread(0)
    part = jnp.zeros((UNITS[1][2], WIDE), jnp.float32)
    arrive(1)
    multiply(1, 0, 96, part)
    collect(1)
    acc = multiply(2, 0, 48, part)
    spread(1)
    multiply(2, 48, 96, acc)
    collect(2)
    scale = finish(0, None)
    spread(2)
    finish(1, scale)
    finish(2, scale)
    out_ref[...] = jnp.maximum(own[...], 0.0)
    for copy in started:
        copy.wait_send()
    for u in range(len(UNITS)):
        for half in range(2):
            swap(u, half).wait_send()
        for dx, dl in others:
            give(u, dx, dl).wait_send()


def on_device(features, adj_tiles, tile_dst, tile_src, tile_count, self_weight, neighbor_weight, layer_bias):
    sends = sum(len(e[3]) for c in range(2) for r in relays(c) for e in r)
    vmem = pl.BlockSpec(memory_space=pltpu.VMEM)
    dma = pltpu.SemaphoreType.DMA
    f32, bf16 = jnp.float32, jnp.bfloat16
    return pl.pallas_call(
        kernel,
        out_shape=jax.ShapeDtypeStruct((TILE, 2 * WIDE), f32),
        in_specs=[pl.BlockSpec(memory_space=pltpu.HBM)] * 8,
        out_specs=vmem,
        scratch_shapes=[
            pltpu.VMEM((NY * NZ, TILE, WIDE), f32),
            pltpu.VMEM((NY * NZ, TILE, WIDE), f32),
            pltpu.VMEM((SLOTS, TILE, TILE), bf16),
            pltpu.VMEM((SLOTS, TILE, WIDE), f32),
            pltpu.VMEM((SLOTS, TILE, TILE), bf16),
            pltpu.VMEM((2, NX * NL, NC, TILE + DEG, WIDE), f32),
            pltpu.VMEM((2, NX * NL, TILE + DEG, WIDE), f32),
            pltpu.VMEM((2, NX * NL, TILE + DEG, WIDE), f32),
            pltpu.VMEM((2, NX * NL, TILE + DEG, WIDE), f32),
            pltpu.VMEM((TILE, 2 * WIDE), f32),
            pltpu.VMEM((2 * WIDE, 2 * WIDE), f32),
            pltpu.VMEM((2 * WIDE, 2 * WIDE), f32),
            pltpu.VMEM((2 * WIDE,), f32),
            pltpu.VMEM((1, SLOTS), jnp.int32),
            pltpu.VMEM((1, SLOTS), jnp.int32),
            pltpu.SMEM((1, 1), jnp.int32),
            pltpu.VMEM((8, 128), jnp.int32),
            pltpu.SMEM((8, 128), jnp.int32),
            dma((sends,)), dma((4 * NY * NZ,)), dma((10,)),
            dma((6,)), dma((6,)), dma((24,)), dma((24,)),
        ],
        compiler_params=pltpu.CompilerParams(
            collective_id=0, has_side_effects=True, vmem_limit_bytes=56 * 1024 * 1024
        ),
        name="sage_layer",
    )(features, adj_tiles, tile_dst, tile_src, tile_count, self_weight, neighbor_weight, layer_bias)


def solution(mesh):
    placed = (
        P(("row", "col"), None),
        P("row", "col", None, None, None),
        P("row", "col", None),
        P("row", "col", None),
        P("row", "col"),
        P(),
        P(),
        P(),
    )
    return jax.shard_map(
        on_device, mesh=mesh, in_specs=placed, out_specs=P(("row", "col"), None), check_vma=False
    )
```

time: 86.7 us -> 73.3 us (0.85)
  Pallas kernels: 78.1 us -> 70.9 us
  local copies, waits for them, and re-layouts: 6.03 us -> 1.57 us
  other arithmetic: 1.15 us -> 0 us
    pallas_call x1, Pallas kernels: 78.1 us -> 70.9 us  [on_device(): pl.pallas_call(kernel, out_shape=jax.ShapeDtypeStruct((TILE, 2 * WIDE), f...]
    unnamed x11 -> x1, local copies, waits for them, and re-layouts: 6.03 us -> 1.57 us
where the time goes in v2:
time: 73.3 us; the launch traced here: 73.2 us
  Pallas kernels  70.9 us (97%)
  local copies, waits for them, and re-layouts  1.57 us (2%)
    pallas_call x1, Pallas kernels, on_device(): pl.pallas_call(kernel, out_shape=jax.ShapeDtypeStruct((TILE, 2 * WIDE), f...  70.9 us
    unnamed x1, local copies, waits for them, and re-layouts  1.57 us

profile of v2, /device:TPU:1, one launch (start us, length us, event | category | flops | bytes accessed | tf_op | source)
XLA Modules:
  0.0 73.2 jit_solution(5043616098496074124)
XLA Ops:
  0.7 70.9 %sage_layer.1 = f32[128,256]{1,0:T(8,128)} custom-call(f32[128,256]{1,0:T(8,128)} %feat_hbm.1, bf16[1,1,96,128,128]{4,3,2,1,0:T(8,128)(2,1)} %adj_hbm.1, s32[1,1,96]{2,1,0:T(1,128)} %dst_hbm.1, s32[1,1,96]{2,1,0:T(1,128)} %src_hbm.1, s32[1,1]{1,0:T(1,128)S(6)} %copy.10.count_hbm, f32[256,256]{1,0:T(8,128)} %ws_hbm.1, f32[256,256]{1,0:T(8,128)} %wn_hbm.1, ...), custom_call_target="tpu_custom_call" | custom-call | tf_op jit(solution)/shard_map/sage_layer/pallas_call | solution.py:326
  71.6 1.6 %copy.11 = f32[128,256]{1,0:T(8,128)} copy(f32[128,256]{1,0:T(8,128)} %sage_layer.1) | data formatting | bytes 262144

commit v3 on v2

--- a/solution.py
+++ b/solution.py
@@ -61,7 +61,7 @@
 def kernel(
     feat_hbm, adj_hbm, dst_hbm, src_hbm, count_hbm, ws_hbm, wn_hbm, bias_hbm, out_ref,
     gath0, gath1, adj, cbuf, abuf, sbuf, got1, mine, got2, own,
-    ws_ref, wn_ref, bias_ref, dst_ref, src_ref, count_ref, rows_ref, table,
+    ws_ref, wn_ref, bias_ref, dst_ref, src_ref, count_ref, rows_ref, table, wide_ref,
     ssem, rsem, in_sem, s1, q1, s2, q2,
 ):
     gath = (gath0, gath1)
@@ -94,12 +94,11 @@
             (bias_hbm, bias_ref),
         ))
     ]
-    for fetch in fetches:
-        fetch.start()
-
     barrier = pltpu.get_barrier_semaphore()
     for peer in peers:
         pl.semaphore_signal(barrier, inc=1, device_id=peer, device_id_type=MESH)
+    for fetch in fetches:
+        fetch.start()
     pl.semaphore_wait(barrier, len(peers))
 
     for fetch in fetches[:2]:
@@ -189,15 +188,24 @@
             preferred_element_type=jnp.float32,
         )
 
+    def both_parts(wide):
+        high = wide.astype(jnp.bfloat16)
+        low = (wide - high.astype(jnp.float32)).astype(jnp.bfloat16)
+        return jnp.concatenate([high, low], axis=1)
+
+    def split(c):
+        def one(s, _):
+            wide_ref[s] = both_parts(gath[c][s])
+            return 0
+
+        lax.fori_loop(0, NY * NZ, one, 0, unroll=4)
+
     def multiply(u, k0, k1, acc):
         c, first, size = UNITS[u]
 
         def step(k, acc):
             key = table[0, k]
-            wide = gath[c][(key >> 7) & 31]
-            high = wide.astype(jnp.bfloat16)
-            low = (wide - high.astype(jnp.float32)).astype(jnp.bfloat16)
-            both = jnp.concatenate([high, low], axis=1)
+            both = both_parts(gath[c][(key >> 7) & 31]) if u < 1 else wide_ref[(key >> 7) & 31]
             tile = adj[key & 127, first : first + size]
             prod = jnp.dot(tile, both, preferred_element_type=jnp.float32)
             acc = jnp.where(is_first(k), 0.0, acc) + (prod[:, :WIDE] + prod[:, WIDE:])
@@ -270,34 +278,39 @@
         )
         return scale
 
+    def sent(u):
+        for half in range(2):
+            swap(u, half).wait_send()
+        for dx, dl in others:
+            give(u, dx, dl).wait_send()
+
     zero = jnp.zeros((TILE, WIDE), jnp.float32)
     relay(0, 0)
     relay(1, 0)
-    tables()
     relay(0, 1)
     relay(1, 1)
+    relay(0, 2)
+    tables()
+    relay(1, 2)
+    acc = sum_tiles(0, 48, zero)
+    relay(0, 3)
+    sum_tiles(48, 96, acc)
+    relay(1, 3)
     own_part()
-    relay(0, 2)
-    acc = sum_tiles(0, 48, zero)
-    relay(1, 2)
-    sum_tiles(48, 96, acc)
-    relay(0, 3)
+    relay(0, 4)
     degrees(0, 8)
-    relay(1, 3)
+    relay(0, 5)
     degrees(8, 16)
-    relay(0, 4)
-    relay(0, 5)
     relay(1, 4)
-    relay(0, 6)
     arrive(0)
-    acc = multiply(0, 0, 48, zero)
+    acc = multiply(0, 0, 32, zero)
     relay(1, 5)
-    multiply(0, 48, 96, acc)
-    relay(1, 6)
+    multiply(0, 32, 96, acc)
     collect(0)
     spread(0)
     part = jnp.zeros((UNITS[1][2], WIDE), jnp.float32)
     arrive(1)
+    split(1)
     multiply(1, 0, 96, part)
     collect(1)
     acc = multiply(2, 0, 48, part)
@@ -306,16 +319,14 @@
     collect(2)
     scale = finish(0, None)
     spread(2)
+    for copy in started:
+        copy.wait_send()
+    sent(0)
     finish(1, scale)
     finish(2, scale)
     out_ref[...] = jnp.maximum(own[...], 0.0)
-    for copy in started:
-        copy.wait_send()
-    for u in range(len(UNITS)):
-        for half in range(2):
-            swap(u, half).wait_send()
-        for dx, dl in others:
-            give(u, dx, dl).wait_send()
+    sent(1)
+    sent(2)
 
 
 def on_device(features, adj_tiles, tile_dst, tile_src, tile_count, self_weight, neighbor_weight, layer_bias):
@@ -323,7 +334,7 @@
     vmem = pl.BlockSpec(memory_space=pltpu.VMEM)
     dma = pltpu.SemaphoreType.DMA
     f32, bf16 = jnp.float32, jnp.bfloat16
-    return pl.pallas_call(
+    summed = pl.pallas_call(
         kernel,
         out_shape=jax.ShapeDtypeStruct((TILE, 2 * WIDE), f32),
         in_specs=[pl.BlockSpec(memory_space=pltpu.HBM)] * 8,
@@ -347,6 +358,7 @@
             pltpu.SMEM((1, 1), jnp.int32),
             pltpu.VMEM((8, 128), jnp.int32),
             pltpu.SMEM((8, 128), jnp.int32),
+            pltpu.VMEM((NY * NZ, TILE, 2 * WIDE), bf16),
             dma((sends,)), dma((4 * NY * NZ,)), dma((10,)),
             dma((6,)), dma((6,)), dma((24,)), dma((24,)),
         ],
@@ -355,6 +367,7 @@
         ),
         name="sage_layer",
     )(features, adj_tiles, tile_dst, tile_src, tile_count, self_weight, neighbor_weight, layer_bias)
+    return summed
 
 
 def solution(mesh):

time: 73.3 us -> 73.1 us (level)
  no operation moved by 1% of the time
where the time goes in v3:
time: 73.1 us; the launch traced here: 73 us
  Pallas kernels  70.8 us (97%)
  local copies, waits for them, and re-layouts  1.57 us (2%)
    pallas_call x1, Pallas kernels, on_device(): pl.pallas_call(kernel, out_shape=jax.ShapeDtypeStruct((TILE, 2 * WIDE), f...  70.8 us
    unnamed x1, local copies, waits for them, and re-layouts  1.57 us

profile of v3, /device:TPU:1, one launch (start us, length us, event | category | flops | bytes accessed | tf_op | source)
XLA Modules:
  0.0 73.0 jit_solution(3408000183437783310)
XLA Ops:
  0.7 70.8 %sage_layer.1 = f32[128,256]{1,0:T(8,128)} custom-call(f32[128,256]{1,0:T(8,128)} %feat_hbm.1, bf16[1,1,96,128,128]{4,3,2,1,0:T(8,128)(2,1)} %adj_hbm.1, s32[1,1,96]{2,1,0:T(1,128)} %dst_hbm.1, s32[1,1,96]{2,1,0:T(1,128)} %src_hbm.1, s32[1,1]{1,0:T(1,128)S(6)} %copy.10.count_hbm, f32[256,256]{1,0:T(8,128)} %ws_hbm.1, f32[256,256]{1,0:T(8,128)} %wn_hbm.1, ...), custom_call_target="tpu_custom_call" | custom-call | tf_op jit(solution)/shard_map/sage_layer/pallas_call | solution.py:337
  71.4 1.6 %copy.11 = f32[128,256]{1,0:T(8,128)} copy(f32[128,256]{1,0:T(8,128)} %sage_layer.1) | data formatting | bytes 262144
